TPU v7x, 512 devices: a whole 4x8x8 slice. The times are simulated.
512 devices in a mesh: seq: 64 (over z, x, core), head: 8 (over y).
Axes of the slice: x: 4, y: 8, z: 8, core: 2. Of those that a mesh axis runs over, the one named last changes fastest.
Arguments:
- queries: float32 [24576, 4096], P('seq', 'head'), may hold values from -1.75 to 1.75
- key_vectors: float32 [24576, 4096], P('seq', 'head'), may hold values from -1.75 to 1.75
- value_vectors: float32 [24576, 4096], P('seq', 'head'), may hold values from -6 to 6
- out_grad: float32 [24576, 4096], P('seq', 'head'), may hold values from -6 to 6
- norm_gain: float32 [4096], P('head'), may hold values from 0.5 to 1.5
- decay_rates: float32 [32], P('head'), may hold values from 4.0690105e-07 to 0.05
- segment_ids: int32 [24576], P('seq'), may hold values from 0 to 5, never falling along the last dimension, each value on 1 to 8192 neighbouring positions
Outputs:
- query_grad: bfloat16 [24576, 4096], P('seq', 'head')
- key_grad: bfloat16 [24576, 4096], P('seq', 'head')
- value_grad: bfloat16 [24576, 4096], P('seq', 'head')
- gain_grad: float32 [4096], P('head')
Inputs may be any that keep to these rules, and one draw needn't show every extreme that they name: `segment_ids`: segment numbers never fall along the tokens; each of the 6 segments is one run of 1 to 8192 tokens, and one has exactly 8192.
All inputs are finite; a program needn't handle non-finite values.
Results may differ from a plain program's by a relative error of at most 0.001.
Values sent between devices are 32-bit elements; how exact they have to be, the bound alone decides.
No kernel may reach another device: no remote copies, remote signals or barrier semaphores. Data moves between devices by JAX's collectives and lax.ppermute only.
A program may use at most 128 MiB of HBM per device.

v0:
```python
import jax
import jax.numpy as jnp
from jax import lax
from jax.sharding import PartitionSpec as P

HEAD_DIM = 128
PRECISE = lax.Precision.HIGHEST
EPSILON = 1e-06


def entering(part, axis, combine, identity, reverse):
    count = lax.axis_size(axis)
    place = lax.axis_index(axis)
    ahead = count - 1 - place if reverse else place
    gathered = jax.tree.map(lambda a: lax.all_gather(a, axis), part)
    state = jax.tree.map(lambda a, e: jnp.zeros_like(a) + jnp.asarray(e, a.dtype), part, identity)

    def one(lap, state):
        source = count - 1 - lap if reverse else lap
        return combine(
            state, jax.tree.map(lambda a: lax.dynamic_index_in_dim(a, source, 0, False), gathered)
        )

    return lax.fori_loop(0, ahead, one, state)


def block_tables(segs, rates):
    length = segs.shape[0]
    places = jnp.arange(length, dtype=jnp.float32)
    first_seg = segs[0]
    last_seg = segs[length - 1]
    distance = places[:, None] - places[None, :]
    causal = (distance >= 0.0) & (segs[:, None] == segs[None, :])
    weights = jnp.where(
        causal[None], jnp.exp(-rates[:, None, None] * jnp.maximum(distance, 0.0)[None]), 0.0
    )
    head_first = (segs == first_seg).astype(jnp.float32)
    tail_last = (segs == last_seg).astype(jnp.float32)
    carry_in_w = jnp.exp(-rates[None, :] * (places[:, None] + 1.0)) * head_first[:, None]
    carry_out_w = jnp.exp(-rates[None, :] * (length - 1.0 - places[:, None])) * tail_last[:, None]
    back_in = jnp.exp(-rates[None, :] * (length - places[:, None])) * tail_last[:, None]
    back_out = jnp.exp(-rates[None, :] * places[:, None]) * head_first[:, None]
    multiplier = jnp.exp(-rates * length) * (first_seg == last_seg).astype(jnp.float32)
    return (weights, carry_in_w, carry_out_w, back_in, back_out, multiplier)


def join_states(earlier, later):
    early_entry, early_exit, early_mult, early_state = earlier
    late_entry, late_exit, late_mult, late_state = later
    keep_flag = ((late_entry == early_exit) | (early_exit < 0.0) | (late_entry < 0.0)).astype(
        jnp.float32
    )
    passed = late_mult * keep_flag
    state_sum = passed[:, None, None] * early_state + late_state
    multiplier = early_mult * passed
    entry_seg = jnp.where(early_entry >= 0.0, early_entry, late_entry)
    exit_seg = jnp.where(late_exit >= 0.0, late_exit, early_exit)
    return (entry_seg, exit_seg, multiplier, state_sum)


def body(queries, key_vectors, value_vectors, out_grad, norm_gain, decay_rates, segment_ids):
    length = queries.shape[0]
    head_count = queries.shape[1] // HEAD_DIM
    features = float(head_count * HEAD_DIM * lax.axis_size("head"))
    query_rows = queries.reshape(length, head_count, HEAD_DIM)
    key_rows = key_vectors.reshape(length, head_count, HEAD_DIM)
    value_rows = value_vectors.reshape(length, head_count, HEAD_DIM)
    weights, carry_in_w, carry_out_w, back_in, back_out, multiplier = block_tables(
        segment_ids, decay_rates
    )
    first_seg = segment_ids[0:1].astype(jnp.float32)
    last_seg = segment_ids[length - 1 : length].astype(jnp.float32)
    zero_state = jnp.zeros((head_count, HEAD_DIM, HEAD_DIM), jnp.float32)
    sentinel = jnp.full((1,), -1.0, jnp.float32)
    identity = (sentinel, sentinel, jnp.ones((head_count,), jnp.float32), zero_state)
    state_loc = jnp.einsum(
        "jhd,jhe->hde", key_rows * carry_out_w[:, :, None], value_rows, precision=PRECISE
    )
    prior_sum = entering(
        (first_seg, last_seg, multiplier, state_loc), "seq", join_states, identity, False
    )
    carry_in = (
        jnp.where(prior_sum[1][0] == first_seg[0], 1.0, 0.0).astype(jnp.float32) * prior_sum[3]
    )
    scores = jnp.einsum("ihd,jhd->hij", query_rows, key_rows, precision=PRECISE) * weights
    outputs = jnp.einsum("hij,jhd->ihd", scores, value_rows, precision=PRECISE)
    outputs = outputs + carry_in_w[:, :, None] * jnp.einsum(
        "ihd,hde->ihe", query_rows, carry_in, precision=PRECISE
    )
    flat_out = outputs.reshape(length, head_count * HEAD_DIM)
    shaped = out_grad * norm_gain[None, :]
    square_part = jnp.sum(flat_out * flat_out, axis=1)
    product_part = jnp.sum(shaped * flat_out, axis=1)
    squares, product = lax.psum((square_part, product_part), "head")
    inv_rms = lax.rsqrt(squares / features + EPSILON)
    coef_rms = inv_rms**3 * (product / features)
    grad_flat = inv_rms[:, None] * shaped - coef_rms[:, None] * flat_out
    gain_part = jnp.sum(out_grad * flat_out * inv_rms[:, None], axis=0)
    gain_grad = lax.psum(gain_part, "seq")
    grad_heads = grad_flat.reshape(length, head_count, HEAD_DIM)
    mixed = jnp.einsum("ihe,jhe->hij", grad_heads, value_rows, precision=PRECISE) * weights
    query_grad = jnp.einsum("hij,jhd->ihd", mixed, key_rows, precision=PRECISE)
    query_grad = query_grad + carry_in_w[:, :, None] * jnp.einsum(
        "ihe,hde->ihd", grad_heads, carry_in, precision=PRECISE
    )
    back_loc = jnp.einsum(
        "thd,the->hde", query_rows * back_out[:, :, None], grad_heads, precision=PRECISE
    )
    later_sum = entering(
        (last_seg, first_seg, multiplier, back_loc), "seq", join_states, identity, True
    )
    carry_back = (
        jnp.where(later_sum[1][0] == last_seg[0], 1.0, 0.0).astype(jnp.float32) * later_sum[3]
    )
    key_grad = jnp.einsum("hij,ihd->jhd", mixed, query_rows, precision=PRECISE)
    key_grad = key_grad + back_in[:, :, None] * jnp.einsum(
        "jhe,hde->jhd", value_rows, carry_back, precision=PRECISE
    )
    value_grad = jnp.einsum("hij,ihe->jhe", scores, grad_heads, precision=PRECISE)
    value_grad = value_grad + back_in[:, :, None] * jnp.einsum(
        "jhd,hde->jhe", key_rows, carry_back, precision=PRECISE
    )
    width = head_count * HEAD_DIM
    return (
        query_grad.reshape(length, width).astype(jnp.bfloat16),
        key_grad.reshape(length, width).astype(jnp.bfloat16),
        value_grad.reshape(length, width).astype(jnp.bfloat16),
        gain_grad,
    )


def solution(mesh):
    return jax.shard_map(
        body,
        mesh=mesh,
        in_specs=(
            P("seq", "head"),
            P("seq", "head"),
            P("seq", "head"),
            P("seq", "head"),
            P("head"),
            P("head"),
            P("seq"),
        ),
        out_specs=(P("seq", "head"), P("seq", "head"), P("seq", "head"), P("head")),
        check_vma=False,
    )
```

profile of v0, /device:TPU:8, one launch (start us, length us, event | category | flops | bytes accessed | tf_op | source)
XLA Modules:
  0.0 1081.8 jit_solution(9144376034380852265)
XLA Ops:
  7.3 1.5 fusion.89
  10.1 2.0 compare_convert_fusion
  12.1 1.4 copy.113
  13.5 1.3 dynamic-slice
  17.0 1.6 fusion.57
  20.9 137.0 %all-reduce.3 = (f32[64]{0:T(128)}, f32[256]{0:T(256)S(1)}, f32[64]{0:T(128)}) all-reduce(f32[64]{0:T(128)S(1)} %convert_dynamic-update-slice_fusion.1, f32[256]{0:T(256)S(1)} %get-tuple-element.272, f32[64]{0:T(128)S(1)} %convert_dynamic-update-slice_fusion), channel_id=2, replica_groups=mesh['seq'=64,'head'=8] {'seq'}, use_global_device_ids=true, to_apply=%add | all-reduce | flops 384 | bytes 3072
  160.1 4.0 fusion.60
  164.1 4.0 fusion.20
  168.2 3.8 multiply_reduce_fusion.2
  171.9 16.8 %psum.21 = f32[384]{0:T(512)} all-reduce(f32[384]{0:T(512)} %get-tuple-element.274), channel_id=1, replica_groups=mesh['seq'=64,'head'=8] {'head'}, use_global_device_ids=true, to_apply=%region_3.4 | all-reduce | flops 384 | bytes 3072 | tf_op jit(solution)/shard_map/psum | solution.py:94
  188.7 2.3 copy.66
  192.3 2.2 multiply_reduce_fusion
  194.5 16.8 %psum.22 = f32[384]{0:T(512)} all-reduce(f32[384]{0:T(512)} %get-tuple-element.222), channel_id=1, replica_groups=mesh['seq'=64,'head'=8] {'head'}, use_global_device_ids=true, to_apply=%region_5.6 | all-reduce | flops 384 | bytes 3072 | tf_op jit(solution)/shard_map/psum | solution.py:94
  212.0 2.5 multiply_subtract_fusion
  214.5 2.3 copy.86
  216.8 3.2 fusion.62
  220.8 4.0 fusion.55
  224.8 3.1 fusion.14
  227.9 1.6 fusion.36
  229.5 1.9 copy.80
  231.4 474.1 %psum.23 = f32[512]{0:T(512)} all-reduce(f32[512]{0:T(512)} %get-tuple-element.221), channel_id=1, replica_groups=mesh['seq'=64,'head'=8] {'seq'}, use_global_device_ids=true, to_apply=%region_9.10 | all-reduce | flops 512 | bytes 4096 | tf_op jit(solution)/shard_map/psum | solution.py:99
  705.5 4.8 fusion.23
  710.3 3.3 fusion.17
  713.7 355.5 %while.33 = (s32[]{:T(128)}, f32[1]{0:T(128)}, f32[4,128,128]{2,1,0:T(8,128)S(1)}, s32[]{:T(128)}, f32[64,1]{0,1:T(1,128)}, /*index=5*/f32[64,4]{1,0:T(8,128)}, ...) while((s32[]{:T(128)}, f32[1]{0:T(128)}, ...), condition=%wide.region_7.8_spmd, body=%wide.region_6.7_spmd.sunk | while | flops 131090 | bytes 786751 | solution.py:24
  713.8 1.3 constant_dynamic-slice_fusion.9
  730.8 1.3 constant_dynamic-slice_fusion.9
  742.1 1.3 constant_dynamic-slice_fusion.9
  759.0 1.3 constant_dynamic-slice_fusion.9
  787.2 1.3 constant_dynamic-slice_fusion.9
  792.9 1.3 constant_dynamic-slice_fusion.9
  1069.2 1.8 fusion.34
  1071.0 1.9 copy.82
  (247 shorter events, 191.6 us)
Async XLA Ops:
  7.2 9.8 copy-start
  7.2 12.1 %copy-start.15 = (s32[384]{0:T(512)S(1)}, s32[384]{0:T(512)}, u32[]{:S(2)}) copy-start(s32[384]{0:T(512)} %param.17) | copy-start | bytes 4612
  7.2 151.4 %copy-start.12 = (f32[384,512]{1,0:T(8,128)S(1)}, f32[384,512]{1,0:T(8,128)}, u32[]{:S(2)}) copy-start(f32[384,512]{1,0:T(8,128)} %param.11) | copy-start | bytes 2359300
  7.2 160.9 %all-gather.8.cloned.1.call-start = ((), (), s32[]{:S(2)}) async-start(), calls=%async_computation | async-start | bytes 17039360 | tf_op jit(solution)/shard_map/all_gather | solution.py:15
  13.5 146.5 %copy-start.8 = (f32[384,512]{0,1:T(8,128)}, f32[384,512]{0,1:T(8,128)S(1)}, u32[]{:S(2)}) copy-start(f32[384,512]{0,1:T(8,128)S(1)} %copy.113) | copy-start | bytes 2359300
  16.3 147.8 %copy-start.16 = (f32[4]{0:T(128)}, f32[4]{0:T(128)S(1)}, u32[]{:S(2)}) copy-start(f32[4]{0:T(128)S(1)} %get-tuple-element.273) | copy-start | bytes 52
  18.6 695.1 %all-gather.10.cloned.1.call-start = ((), (), s32[]{:S(2)}) async-start(), calls=%async_computation.1 | async-start | bytes 17039360 | tf_op jit(solution)/shard_map/all_gather | solution.py:15
  159.8 4.3 copy-start.5
  191.7 0.6 copy-start.18
  220.7 4.0 copy-start.6
  220.7 4.0 copy-start.9
  220.7 4.0 copy-start.17
  224.7 4.7 copy-start.1
  224.8 3.1 copy-start.4
  224.8 3.1 copy-start.14
  705.5 4.8 copy-start.2
  705.5 4.8 copy-start.3
  705.5 4.8 copy-start.7
  710.3 358.9 %copy-start.11 = (f32[384,4,128]{0,2,1:T(8,128)S(1)}, f32[384,4,128]{0,2,1:T(8,128)}, u32[]{:S(2)}) copy-start(f32[384,4,128]{0,2,1:T(8,128)} %fusion.23) | copy-start | bytes 2359300
  713.7 355.6 %copy-start.10 = (f32[384,512]{1,0:T(8,128)S(1)}, f32[384,512]{1,0:T(8,128)}, u32[]{:S(2)}) copy-start(f32[384,512]{1,0:T(8,128)} %param.12) | copy-start | bytes 2359300
  713.7 355.6 %copy-start.13 = (f32[384,4]{0,1:T(4,128)S(1)}, f32[384,4]{0,1:T(4,128)}, u32[]{:S(2)}) copy-start(f32[384,4]{0,1:T(4,128)} %get-tuple-element.271) | copy-start | bytes 18436
Sparse Core Ops, SparseCore 0:
  18.7 110.4 all-gather.7
  220.2 444.5 all-gather.9
where the time goes:
time: 1090 us; the launch traced here: 1080 us
  blocking collectives  645 us (59%)
  loops' own time  166 us (15%)
  other arithmetic  121 us (11%)
  local copies, waits for them, and re-layouts  96.1 us (9%)
  matrix products  36.2 us (3%)
  between operations  17.8 us (2%)
    psum x1, blocking collectives, body(): gain_grad = lax.psum(gain_part, 'seq')  474 us
    another operation x2, loops' own time, entering(): return lax.fori_loop(0, ahead, one, state)  166 us
    unnamed x1, blocking collectives  137 us
    dynamic_slice x63, local copies, waits for them, and re-layouts, one(): lax.dynamic_index_in_dim(a, source, 0, False)  80 us
    add x63, other arithmetic, join_states(): state_sum = passed[:, None, None] * early_state + late_state  66.4 us
    mul x63, other arithmetic, join_states(): passed = late_mult * keep_flag  43.5 us
    psum x2, blocking collectives, body(): squares, product = lax.psum((square_part, product_part), 'head')  33.6 us
  transfers between devices with their start and end apart: 2, of which 0 were waited for; matrix products, arithmetic and copies ran while one was open for 3% of the time, Pallas kernels for 0%

commit v1 on v0

--- a/solution.py
+++ b/solution.py
@@ -96,7 +96,8 @@
     coef_rms = inv_rms**3 * (product / features)
     grad_flat = inv_rms[:, None] * shaped - coef_rms[:, None] * flat_out
     gain_part = jnp.sum(out_grad * flat_out * inv_rms[:, None], axis=0)
-    gain_grad = lax.psum(gain_part, "seq")
+    blocks = lax.all_gather(gain_part, "seq", axis=0, tiled=False)
+    gain_grad = blocks.sum(axis=0)
     grad_heads = grad_flat.reshape(length, head_count, HEAD_DIM)
     mixed = jnp.einsum("ihe,jhe->hij", grad_heads, value_rows, precision=PRECISE) * weights
     query_grad = jnp.einsum("hij,jhd->ihd", mixed, key_rows, precision=PRECISE)

time: 1090 us -> 1040 us (0.954)
  blocking collectives: 645 us -> 563 us
  waiting for transfers between devices: 0.05 us -> 32.5 us
    psum x1 -> x0, blocking collectives: 474 us -> none  [body(): gain_grad = lax.psum(gain_part, 'seq')]
    all_gather x0 -> x1, blocking collectives: none -> 392 us  [body(): blocks = lax.all_gather(gain_part, 'seq', axis=0, tiled=False)]
    all_gather x2, waiting for transfers between devices: 0.02 us -> 32.4 us  [entering(): gathered = jax.tree.map(lambda a: lax.all_gather(a, axis), part)]
  transfers between devices with their start and end apart: 2 -> 2, of which waited for: 0 -> 1; matrix products, arithmetic and copies ran while one was open for 3% -> 3% of each run, Pallas kernels for 0% -> 0%
where the time goes in v1:
time: 1040 us; the launch traced here: 1030 us
  blocking collectives  563 us (54%)
  loops' own time  166 us (16%)
  other arithmetic  122 us (12%)
  local copies, waits for them, and re-layouts  95.9 us (9%)
  matrix products  35.7 us (3%)
  waiting for transfers between devices  32.5 us (3%)
  between operations  17.7 us (2%)
    all_gather x1, blocking collectives, body(): blocks = lax.all_gather(gain_part, 'seq', axis=0, tiled=False)  392 us
    another operation x2, loops' own time, entering(): return lax.fori_loop(0, ahead, one, state)  166 us
    unnamed x1, blocking collectives  137 us
    dynamic_slice x63, local copies, waits for them, and re-layouts, one(): lax.dynamic_index_in_dim(a, source, 0, False)  79.8 us
    add x63, other arithmetic, join_states(): state_sum = passed[:, None, None] * early_state + late_state  66.4 us
    mul x63, other arithmetic, join_states(): passed = late_mult * keep_flag  43.5 us
    psum x2, blocking collectives, body(): squares, product = lax.psum((square_part, product_part), 'head')  33.6 us
    all_gather x2, waiting for transfers between devices, entering(): gathered = jax.tree.map(lambda a: lax.all_gather(a, axis), part)  32.4 us
  transfers between devices with their start and end apart: 2, of which 1 were waited for; matrix products, arithmetic and copies ran while one was open for 3% of the time, Pallas kernels for 0%

profile of v1, /device:TPU:8, one launch (start us, length us, event | category | flops | bytes accessed | tf_op | source)
XLA Modules:
  0.0 1032.3 jit_solution(8861589623123865702)
XLA Ops:
  7.3 1.5 fusion.89
  10.1 2.0 compare_convert_fusion
  12.1 1.4 copy.113
  13.5 1.3 dynamic-slice
  16.9 1.6 fusion.57
  20.9 137.0 %all-reduce.3 = (f32[64]{0:T(128)}, f32[256]{0:T(256)S(1)}, f32[64]{0:T(128)}) all-reduce(f32[64]{0:T(128)S(1)} %convert_dynamic-update-slice_fusion.1, f32[256]{0:T(256)S(1)} %get-tuple-element.272, f32[64]{0:T(128)S(1)} %convert_dynamic-update-slice_fusion), channel_id=2, replica_groups=mesh['seq'=64,'head'=8] {'seq'}, use_global_device_ids=true, to_apply=%add | all-reduce | flops 384 | bytes 3072
  160.0 4.0 fusion.60
  164.1 4.0 fusion.20
  168.1 3.8 multiply_reduce_fusion.2
  171.9 16.8 %psum.14 = f32[384]{0:T(512)} all-reduce(f32[384]{0:T(512)} %get-tuple-element.274), channel_id=1, replica_groups=mesh['seq'=64,'head'=8] {'head'}, use_global_device_ids=true, to_apply=%region_3.4 | all-reduce | flops 384 | bytes 3072 | tf_op jit(solution)/shard_map/psum | solution.py:94
  188.7 2.3 copy.66
  192.3 2.2 multiply_reduce_fusion
  194.5 16.8 %psum.15 = f32[384]{0:T(512)} all-reduce(f32[384]{0:T(512)} %get-tuple-element.222), channel_id=1, replica_groups=mesh['seq'=64,'head'=8] {'head'}, use_global_device_ids=true, to_apply=%region_5.6 | all-reduce | flops 384 | bytes 3072 | tf_op jit(solution)/shard_map/psum | solution.py:94
  212.0 2.4 multiply_subtract_fusion
  214.4 2.3 copy.86
  216.7 3.2 fusion.62
  220.7 4.0 fusion.55
  224.7 3.1 fusion.14
  227.8 1.6 fusion.36
  229.4 1.9 copy.80
  231.3 392.4 %all-gather.6 = f32[64,1,512]{2,1,0:T(1,128)S(1)} all-gather(f32[1,1,512]{2,1,0:T(1,128)} %bitcast.150), channel_id=7, replica_groups=mesh['seq'=64,'head'=8] {'seq'}, dimensions={0}, use_global_device_ids=true | all-gather | bytes 133120 | tf_op jit(solution)/shard_map/all_gather | solution.py:99
  624.4 5.0 fusion.23
  629.4 2.6 fusion.17
  632.1 32.4 %all-gather.12.cloned.1.call-done = f32[256,128,128]{2,1,0:T(8,128)} async-done(((f32[4,128,128]{2,1,0:T(8,128)}), f32[256,128,128]{2,1,0:T(8,128)}) %all-gather.12.cloned.1.call-update) | async-done | bytes 16777232 | tf_op jit(solution)/shard_map/all_gather | solution.py:15
  664.5 355.2 %while.33 = (s32[]{:T(128)}, f32[1]{0:T(128)}, f32[4,128,128]{2,1,0:T(8,128)S(1)}, s32[]{:T(128)}, f32[64,1]{0,1:T(1,128)}, /*index=5*/f32[64,4]{1,0:T(8,128)}, ...) while((s32[]{:T(128)}, f32[1]{0:T(128)}, ...), condition=%wide.region_7.8_spmd, body=%wide.region_6.7_spmd.sunk | while | flops 131090 | bytes 786751 | solution.py:24
  698.4 1.3 constant_dynamic-slice_fusion.9
  788.6 1.3 constant_dynamic-slice_fusion.9
  884.5 1.3 constant_dynamic-slice_fusion.9
  918.4 1.3 constant_dynamic-slice_fusion.9
  946.6 1.3 constant_dynamic-slice_fusion.9
  1019.8 1.8 fusion.34
  1021.6 1.9 copy.82
  (250 shorter events, 193.4 us)
Async XLA Ops:
  7.2 9.8 copy-start
  7.2 12.1 %copy-start.15 = (s32[384]{0:T(512)S(1)}, s32[384]{0:T(512)}, u32[]{:S(2)}) copy-start(s32[384]{0:T(512)} %param.17) | copy-start | bytes 4612
  7.2 151.4 %copy-start.12 = (f32[384,512]{1,0:T(8,128)S(1)}, f32[384,512]{1,0:T(8,128)}, u32[]{:S(2)}) copy-start(f32[384,512]{1,0:T(8,128)} %param.11) | copy-start | bytes 2359300
  7.2 160.9 %all-gather.10.cloned.1.call-start = ((), (), s32[]{:S(2)}) async-start(), calls=%async_computation | async-start | bytes 17039360 | tf_op jit(solution)/shard_map/all_gather | solution.py:15
  13.5 146.5 %copy-start.8 = (f32[384,512]{0,1:T(8,128)}, f32[384,512]{0,1:T(8,128)S(1)}, u32[]{:S(2)}) copy-start(f32[384,512]{0,1:T(8,128)S(1)} %copy.113) | copy-start | bytes 2359300
  16.2 147.8 %copy-start.16 = (f32[4]{0:T(128)}, f32[4]{0:T(128)S(1)}, u32[]{:S(2)}) copy-start(f32[4]{0:T(128)S(1)} %get-tuple-element.273) | copy-start | bytes 52
  18.6 645.9 %all-gather.12.cloned.1.call-start = ((), (), s32[]{:S(2)}) async-start(), calls=%async_computation.1 | async-start | bytes 17039360 | tf_op jit(solution)/shard_map/all_gather | solution.py:15
  159.8 4.3 copy-start.5
  191.7 0.6 copy-start.19
  220.7 4.0 copy-start.6
  220.7 4.0 copy-start.9
  220.7 4.0 copy-start.17
  224.7 4.7 copy-start.1
  224.7 3.1 copy-start.4
  224.7 3.1 copy-start.14
  624.4 5.0 copy-start.2
  624.4 5.0 copy-start.3
  624.4 5.0 copy-start.7
  624.4 5.0 copy-start.18
  629.4 390.4 %copy-start.11 = (f32[384,4,128]{0,2,1:T(8,128)S(1)}, f32[384,4,128]{0,2,1:T(8,128)}, u32[]{:S(2)}) copy-start(f32[384,4,128]{0,2,1:T(8,128)} %fusion.23) | copy-start | bytes 2359300
  632.1 387.7 %copy-start.10 = (f32[384,512]{1,0:T(8,128)S(1)}, f32[384,512]{1,0:T(8,128)}, u32[]{:S(2)}) copy-start(f32[384,512]{1,0:T(8,128)} %param.12) | copy-start | bytes 2359300
  632.1 387.7 %copy-start.13 = (f32[384,4]{0,1:T(4,128)S(1)}, f32[384,4]{0,1:T(4,128)}, u32[]{:S(2)}) copy-start(f32[384,4]{0,1:T(4,128)} %get-tuple-element.271) | copy-start | bytes 18436
Sparse Core Ops, SparseCore 0:
  18.7 110.4 all-gather.9
  220.1 444.3 all-gather.11
